TPU v7x, 512 devices: a whole 4x4x16 slice. The times are simulated.
512 devices in a mesh: dp: 32 (over x_hi, z), tm: 16 (over y, x_lo, core).
Axes of the slice: x: 4 (x_hi: 2, x_lo: 2; x = x_hi * 2 + x_lo), y: 4, z: 16, core: 2. Of those that a mesh axis runs over, the one named last changes fastest.
Arguments:
- clip_input: bfloat16 [32, 32, 256, 384], P('dp', 'tm'), may hold values from -32 to 32
- norm_gain: float32 [384], replicated, may hold values from 0.1 to 1.9
- qkv_weight: bfloat16 [384, 1152], replicated, may hold values from -2 to 2
- out_weight: bfloat16 [384, 384], replicated, may hold values from -0.3125 to 0.3125
- time_weight: bfloat16 [3, 384, 768], P(None, 'dp'), may hold values from -0.1875 to 0.1875
- upsample_cotangent: bfloat16 [32, 32, 256, 768], P('dp', 'tm'), may hold values from -6 to 6
Outputs:
- input_grad: bfloat16 [32, 32, 256, 384], P('dp', 'tm')
- qkv_grad: float32 [384, 1152], P('dp', 'tm')
All inputs are finite; a program needn't handle non-finite values.
Results may differ from a plain program's by a relative error of at most 0.024.
Values may be sent and summed in bfloat16 or wider, within the bound.
No kernel may reach another device: no remote copies, remote signals or barrier semaphores. Data moves between devices by JAX's collectives and lax.ppermute only.
A program may use at most 64 MiB of HBM per device.

v0:
```python
import math
import jax
import jax.numpy as jnp
from jax import lax
from jax.sharding import PartitionSpec as P


def passed_along(block, axis, distance):
    devices = range(lax.axis_size(axis))
    route = [(i - distance, i) for i in devices if i - distance in devices]
    return lax.ppermute(block, axis, route)


def rms_scaled(features, norm_gain):
    squares = jnp.mean(features * features, axis=-1, keepdims=True)
    return features * lax.rsqrt(squares + 1e-06) * norm_gain


def block_tail(qkv_rows, features, out_weight):
    width = features.shape[-1]
    queries = qkv_rows[..., :width]
    keys = qkv_rows[..., width : 2 * width]
    values = qkv_rows[..., 2 * width :]
    scores = jnp.einsum(
        "fqc,fkc->fqk", queries, keys, preferred_element_type=jnp.float32
    ) / math.sqrt(width)
    weights = jax.nn.softmax(scores, axis=-1).astype(jnp.bfloat16)
    mixed = jnp.einsum("fqk,fkc->fqc", weights, values, preferred_element_type=jnp.float32).astype(
        jnp.bfloat16
    )
    branch = jnp.einsum("fqc,cd->fqd", mixed, out_weight, preferred_element_type=jnp.float32)
    return (features + branch).astype(jnp.bfloat16)


def attention_grads(clip_rows, norm_gain, qkv_weight, out_weight, upstream):
    features = clip_rows.astype(jnp.float32)
    normed, pre_back = jax.vjp(lambda value: rms_scaled(value, norm_gain), features)
    normed_bf = normed.astype(jnp.bfloat16)
    qkv_rows = jnp.einsum(
        "fhc,cd->fhd", normed_bf, qkv_weight, preferred_element_type=jnp.float32
    ).astype(jnp.bfloat16)
    block_out, tail_back = jax.vjp(
        lambda first, second: block_tail(first, second, out_weight), qkv_rows, features
    )
    qkv_cot, feature_cot = tail_back(upstream)
    normed_cot = jnp.einsum("fhd,cd->fhc", qkv_cot, qkv_weight, preferred_element_type=jnp.float32)
    direct = pre_back(normed_cot)[0]
    input_grad = (feature_cot + direct).astype(jnp.bfloat16)
    return (input_grad, normed_bf, qkv_cot)


def on_device(clip_input, norm_gain, qkv_weight, out_weight, time_weight, upsample_cotangent):
    rows = clip_input[0]
    cotangent = upsample_cotangent[0]
    frames = cotangent.shape[0]
    width = rows.shape[-1]
    incoming = passed_along(cotangent, "tm", -1)
    padded = jnp.concatenate([cotangent, incoming], 0)
    piece = lax.all_gather(time_weight, "dp", axis=1, tiled=True)
    result = jnp.einsum(
        "fhd,cd->fhc", padded[2 : 2 + frames], piece[0], preferred_element_type=jnp.float32
    )
    result = result + jnp.einsum(
        "fhd,cd->fhc", padded[1 : 1 + frames], piece[1], preferred_element_type=jnp.float32
    )
    upstream = (
        result
        + jnp.einsum("fhd,cd->fhc", padded[0:frames], piece[2], preferred_element_type=jnp.float32)
    ).astype(jnp.bfloat16)
    input_grad, normed_bf, qkv_cot = attention_grads(
        rows, norm_gain, qkv_weight, out_weight, upstream
    )
    flat_normed = normed_bf.reshape(-1, width)
    flat_cot = qkv_cot.reshape(-1, 3 * width)
    shares = lax.psum_scatter(
        jnp.einsum("rc,rd->cd", flat_normed, flat_cot, preferred_element_type=jnp.float32).astype(
            jnp.bfloat16
        ),
        "dp",
        scatter_dimension=0,
        tiled=True,
    )
    qkv_grad = lax.psum_scatter(shares, "tm", scatter_dimension=1, tiled=True).astype(jnp.float32)
    return (input_grad[None], qkv_grad)


def solution(mesh):
    in_specs = (
        P("dp", "tm", None, None),
        P(),
        P(),
        P(),
        P(None, "dp", None),
        P("dp", "tm", None, None),
    )
    out_specs = (P("dp", "tm", None, None), P("dp", "tm"))
    return jax.shard_map(
        on_device, mesh=mesh, in_specs=in_specs, out_specs=out_specs, check_vma=False
    )
```

profile of v0, /device:TPU:4, one launch (start us, length us, event | category | flops | bytes accessed | tf_op | source)
XLA Modules:
  0.0 387.8 jit_solution(9534692791571639131)
XLA Ops:
  7.2 1.6 copy.10
  15.2 1.9 convolution_convert_fusion
  18.1 147.2 %all-gather.2.cloned.1.call-done = bf16[3,384,768]{2,0,1:T(4,128)(2,1)} async-done(((bf16[3,12,768]{2,0,1:T(4,128)(2,1)}), bf16[3,384,768]{2,0,1:T(4,128)(2,1)}) %all-gather.2.cloned.1.call-update) | async-done | bytes 1769488 | tf_op jit(solution)/shard_map/all_gather | solution.py:59
  165.3 6.4 %fusion.37 = (bf16[1,384,768]{2,0,1:T(2,128)(2,1)S(1)}, bf16[1,384,768]{2,0,1:T(2,128)(2,1)S(1)}, bf16[1,384,768]{2,0,1:T(2,128)(2,1)S(1)}) fusion(bf16[3,384,768]{2,0,1:T(4,128)(2,1)} %all-gather.2.cloned.1.call-done), kind=kLoop, calls=%fused_computation.61 | loop fusion | bytes 3538944 | tf_op jit(solution)/shard_map/slice | solution.py:61
  172.4 1.6 fusion.3
  174.0 1.8 fusion.9
  177.5 2.1 convolution_convert_fusion.2
  179.7 2.2 convolution_convert_fusion.1
  183.0 1.9 fusion.2
  184.9 84.6 %fusion = bf16[16,1152]{1,0:T(8,128)(2,1)S(1)} fusion(bf16[384,1152]{1,0:T(8,128)(2,1)S(1)} %fusion.2), kind=kCustom, calls=%all-reduce-scatter | all-reduce-scatter fusion | flops 589825 | bytes 923648
  269.5 1.9 collective-permute-start.1
  271.4 1.9 collective-permute-start.2
  273.3 1.9 collective-permute-start.3
  275.3 1.9 collective-permute-start.4
  277.2 2.0 fusion.19
  279.2 8.9 %collective-permute-start.8 = (bf16[12,1152]{1,0:T(8,128)(2,1)S(1)}, bf16[12,1152]{1,0:T(8,128)(2,1)S(1)}, u32[]{:S(2)}, u32[]{:S(2)}) collective-permute-start(bf16[12,1152]{1,0:T(8,128)(2,1)S(1)} %slice.34), channel_id=1, source_target_pairs={{0,128},{16,144},{32,160},{48,176},{64,192},{80,208},{96,224},{112... | collective-permute-start | bytes 82952
  288.2 9.5 %collective-permute-done.8 = bf16[12,1152]{1,0:T(8,128)(2,1)S(1)} collective-permute-done((bf16[12,1152]{1,0:T(8,128)(2,1)S(1)}, bf16[12,1152]{1,0:T(8,128)(2,1)S(1)}, u32[]{:S(2)}, u32[]{:S(2)}) %collective-permute-start.8) | collective-permute-done | bytes 27680
  297.7 8.0 %collective-permute-start.5 = (bf16[16,1152]{1,0:T(8,128)(2,1)S(1)}, bf16[16,1152]{1,0:T(8,128)(2,1)S(1)}, u32[]{:S(2)}, u32[]{:S(2)}) collective-permute-start(bf16[16,1152]{1,0:T(8,128)(2,1)S(1)} %fusion), channel_id=1, source_target_pairs={{0,80},{16,96},{32,112},{48,128},{64,144},{80,160},{96,176},{112,1... | collective-permute-start | bytes 110600
  305.7 3.3 collective-permute-start.6
  309.0 1.9 collective-permute-start.7
  312.0 9.4 %collective-permute-done.6 = bf16[16,1152]{1,0:T(8,128)(2,1)S(1)} collective-permute-done((bf16[16,1152]{1,0:T(8,128)(2,1)S(1)}, bf16[16,1152]{1,0:T(8,128)(2,1)S(1)}, u32[]{:S(2)}, u32[]{:S(2)}) %collective-permute-start.6) | collective-permute-done | bytes 36896
  321.4 4.5 %collective-permute-done.7 = bf16[16,1152]{1,0:T(8,128)(2,1)S(1)} collective-permute-done((bf16[16,1152]{1,0:T(8,128)(2,1)S(1)}, bf16[16,1152]{1,0:T(8,128)(2,1)S(1)}, u32[]{:S(2)}, u32[]{:S(2)}) %collective-permute-start.7) | collective-permute-done | bytes 36896
  325.9 1.5 concatenate.4
  327.4 53.0 %all-reduce.4 = bf16[12,1152]{1,0:T(8,128)(2,1)S(1)} all-reduce(bf16[12,1152]{1,0:T(8,128)(2,1)S(1)} %constant_dynamic-slice_fusion), channel_id=3, replica_groups=mesh['dp'=32,'tm'=16] {'tm'}, use_global_device_ids=true, to_apply=%region_6.0.clone | all-reduce | flops 13824 | bytes 55296
  (40 shorter events, 11.3 us)
Async XLA Ops:
  7.2 8.0 %copy-start = (bf16[384,1152]{1,0:T(8,128)(2,1)S(1)}, bf16[384,1152]{1,0:T(8,128)(2,1)}, u32[]{:S(2)}) copy-start(bf16[384,1152]{1,0:T(8,128)(2,1)} %param.8) | copy-start | bytes 2654212
  7.2 158.1 %all-gather.2.cloned.1.call-start = ((), (), s32[]{:S(2)}) async-start(), calls=%async_computation | async-start | bytes 2433024 | tf_op jit(solution)/shard_map/all_gather | solution.py:59
  8.9 163.5 %collective-permute-start = (bf16[2,256,768]{2,1,0:T(8,128)(2,1)}, bf16[2,256,768]{2,1,0:T(8,128)(2,1)}, u32[]{:S(2)}, u32[]{:S(2)}) collective-permute-start(bf16[2,256,768]{2,1,0:T(8,128)(2,1)} %bitcast.53), channel_id=1, source_target_pairs={{1,0},{2,1},{3,2},{4,3},{5,4},{6,5},{7,6},{8,7},{9,8},{10,9},{11,1... | collective-permute-start | bytes 2359304 | tf_op jit(solution)/shard_map/ppermute | solution.py:11
  17.1 1.0 copy-start.2
  18.1 153.6 %copy-start.3 = (bf16[1,2,256,768]{3,2,1,0:T(8,128)(2,1)S(1)}, bf16[1,2,256,768]{3,2,1,0:T(8,128)(2,1)}, u32[]{:S(2)}) copy-start(bf16[1,2,256,768]{3,2,1,0:T(8,128)(2,1)} %param.11) | copy-start | bytes 2359300
  174.0 1.8 copy-start.4
  181.8 1.1 copy-start.1
  181.8 1.1 copy-start.5
  181.8 1.1 copy-start.6
  269.5 36.2 %collective-permute-start.1 = (bf16[16,1152]{1,0:T(8,128)(2,1)S(1)}, bf16[16,1152]{1,0:T(8,128)(2,1)S(1)}, u32[]{:S(2)}, u32[]{:S(2)}) collective-permute-start(bf16[16,1152]{1,0:T(8,128)(2,1)S(1)} %fusion), channel_id=1, source_target_pairs={{0,16},{16,32},{32,48},{48,64},{64,80},{80,96},{96,112},{112,128},... | collective-permute-start | bytes 110600
  271.4 37.6 %collective-permute-start.2 = (bf16[16,1152]{1,0:T(8,128)(2,1)S(1)}, bf16[16,1152]{1,0:T(8,128)(2,1)S(1)}, u32[]{:S(2)}, u32[]{:S(2)}) collective-permute-start(bf16[16,1152]{1,0:T(8,128)(2,1)S(1)} %fusion), channel_id=1, source_target_pairs={{0,32},{16,48},{32,64},{48,80},{64,96},{80,112},{96,128},{112,144}... | collective-permute-start | bytes 110600
  273.3 38.6 %collective-permute-start.3 = (bf16[16,1152]{1,0:T(8,128)(2,1)S(1)}, bf16[16,1152]{1,0:T(8,128)(2,1)S(1)}, u32[]{:S(2)}, u32[]{:S(2)}) collective-permute-start(bf16[16,1152]{1,0:T(8,128)(2,1)S(1)} %fusion), channel_id=1, source_target_pairs={{0,48},{16,64},{32,80},{48,96},{64,112},{80,128},{96,144},{112,160... | collective-permute-start | bytes 110600
  275.3 36.7 %collective-permute-start.4 = (bf16[16,1152]{1,0:T(8,128)(2,1)S(1)}, bf16[16,1152]{1,0:T(8,128)(2,1)S(1)}, u32[]{:S(2)}, u32[]{:S(2)}) collective-permute-start(bf16[16,1152]{1,0:T(8,128)(2,1)S(1)} %fusion), channel_id=1, source_target_pairs={{0,64},{16,80},{32,96},{48,112},{64,128},{80,144},{96,160},{112,17... | collective-permute-start | bytes 110600
  279.2 18.5 %collective-permute-start.8 = (bf16[12,1152]{1,0:T(8,128)(2,1)S(1)}, bf16[12,1152]{1,0:T(8,128)(2,1)S(1)}, u32[]{:S(2)}, u32[]{:S(2)}) collective-permute-start(bf16[12,1152]{1,0:T(8,128)(2,1)S(1)} %slice.34), channel_id=1, source_target_pairs={{0,128},{16,144},{32,160},{48,176},{64,192},{80,208},{96,224},{112... | collective-permute-start | bytes 82952
  297.7 14.3 %collective-permute-start.5 = (bf16[16,1152]{1,0:T(8,128)(2,1)S(1)}, bf16[16,1152]{1,0:T(8,128)(2,1)S(1)}, u32[]{:S(2)}, u32[]{:S(2)}) collective-permute-start(bf16[16,1152]{1,0:T(8,128)(2,1)S(1)} %fusion), channel_id=1, source_target_pairs={{0,80},{16,96},{32,112},{48,128},{64,144},{80,160},{96,176},{112,1... | collective-permute-start | bytes 110600
  305.7 15.7 %collective-permute-start.6 = (bf16[16,1152]{1,0:T(8,128)(2,1)S(1)}, bf16[16,1152]{1,0:T(8,128)(2,1)S(1)}, u32[]{:S(2)}, u32[]{:S(2)}) collective-permute-start(bf16[16,1152]{1,0:T(8,128)(2,1)S(1)} %fusion), channel_id=1, source_target_pairs={{0,96},{16,112},{32,128},{48,144},{64,160},{80,176},{96,192},{112,... | collective-permute-start | bytes 110600
  309.0 16.9 %collective-permute-start.7 = (bf16[16,1152]{1,0:T(8,128)(2,1)S(1)}, bf16[16,1152]{1,0:T(8,128)(2,1)S(1)}, u32[]{:S(2)}, u32[]{:S(2)}) collective-permute-start(bf16[16,1152]{1,0:T(8,128)(2,1)S(1)} %fusion), channel_id=1, source_target_pairs={{0,112},{16,128},{32,144},{48,160},{64,176},{80,192},{96,208},{112... | collective-permute-start | bytes 110600
Sparse Core Ops, SparseCore 0:
  11.7 153.5 all-gather.1
where the time goes:
time: 389 us; the launch traced here: 388 us
  waiting for transfers between devices  171 us (44%)
  blocking collectives  138 us (35%)
  starting transfers between devices  31.1 us (8%)
  matrix products  17.3 us (4%)
  between operations  15.6 us (4%)
  local copies, waits for them, and re-layouts  12.4 us (3%)
    all_gather x1, waiting for transfers between devices, on_device(): piece = lax.all_gather(time_weight, 'dp', axis=1, tiled=True)  147 us
    unnamed x2, blocking collectives  138 us
    unnamed x8, starting transfers between devices  29.8 us
    unnamed x9, waiting for transfers between devices  23.5 us
  transfers between devices with their start and end apart: 10, of which 4 were waited for; matrix products, arithmetic and copies ran while one was open for 4% of the time, Pallas kernels for 0%

commit v1 on v0

--- a/solution.py
+++ b/solution.py
@@ -56,7 +56,15 @@
     width = rows.shape[-1]
     incoming = passed_along(cotangent, "tm", -1)
     padded = jnp.concatenate([cotangent, incoming], 0)
-    piece = lax.all_gather(time_weight, "dp", axis=1, tiled=True)
+    piece = jnp.concatenate(
+        lax.all_to_all(
+            jnp.stack([time_weight for _ in range(lax.psum(1, axis_name="dp"))], axis=0),
+            axis_name="dp",
+            split_axis=0,
+            concat_axis=0,
+        ),
+        axis=1,
+    )
     result = jnp.einsum(
         "fhd,cd->fhc", padded[2 : 2 + frames], piece[0], preferred_element_type=jnp.float32
     )

time: 389 us -> 345 us (0.89)
  waiting for transfers between devices: 171 us -> 116 us
  starting transfers between devices: 31.1 us -> 54.6 us
  between operations: 15.6 us -> 2.3 us
    all_gather x1 -> x0, waiting for transfers between devices: 147 us -> none  [on_device(): piece = lax.all_gather(time_weight, 'dp', axis=1, tiled=True)]
    all_to_all x0 -> x1, waiting for transfers between devices: none -> 95.4 us  [on_device(): lax.all_to_all(jnp.stack([time_weight for _ in range(lax.psum(1, axis_nam...]
    all_to_all x0 -> x1, starting transfers between devices: none -> 18.4 us  [on_device(): lax.all_to_all(jnp.stack([time_weight for _ in range(lax.psum(1, axis_nam...]
    unnamed x8, starting transfers between devices: 29.8 us -> 35 us
    slice x1, local copies, waits for them, and re-layouts: 6.43 us -> 1.47 us  [on_device(): piece[0]]
    unnamed x9 -> x8, waiting for transfers between devices: 23.5 us -> 20.1 us
  transfers between devices with their start and end apart: 10 -> 10, of which waited for: 4 -> 4; matrix products, arithmetic and copies ran while one was open for 4% -> 5% of each run, Pallas kernels for 0% -> 0%
where the time goes in v1:
time: 345 us; the launch traced here: 344 us
  blocking collectives  138 us (40%)
  waiting for transfers between devices  116 us (34%)
  starting transfers between devices  54.6 us (16%)
  matrix products  19.2 us (6%)
  local copies, waits for them, and re-layouts  11.1 us (3%)
  other arithmetic  3.94 us (1%)
    unnamed x2, blocking collectives  138 us
    all_to_all x1, waiting for transfers between devices, on_device(): lax.all_to_all(jnp.stack([time_weight for _ in range(lax.psum(1, axis_nam...  95.4 us
    unnamed x8, starting transfers between devices  35 us
    unnamed x8, waiting for transfers between devices  20.1 us
    all_to_all x1, starting transfers between devices, on_device(): lax.all_to_all(jnp.stack([time_weight for _ in range(lax.psum(1, axis_nam...  18.4 us
  transfers between devices with their start and end apart: 10, of which 4 were waited for; matrix products, arithmetic and copies ran while one was open for 5% of the time, Pallas kernels for 0%

profile of v1, /device:TPU:4, one launch (start us, length us, event | category | flops | bytes accessed | tf_op | source)
XLA Modules:
  0.0 344.5 jit_solution(7390792135793071628)
XLA Ops:
  0.6 2.5 stack.2
  3.2 18.4 %all-to-all-start = ((bf16[32,3,12,768]{3,2,1,0:T(8,128)(2,1)}), bf16[32,3,12,768]{3,2,1,0:T(8,128)(2,1)S(1)}, u32[]{:S(2)}, u32[]{:S(2)}) async-start(bf16[32,3,12,768]{3,2,1,0:T(8,128)(2,1)} %stack.2), calls=%async_computation | async-start | bytes 4718592 | tf_op jit(solution)/shard_map/all_to_all | solution.py:60
  27.9 1.9 convolution_convert_fusion
  31.2 95.4 %all-to-all-done = bf16[32,3,12,768]{3,2,1,0:T(8,128)(2,1)S(1)} async-done(((bf16[32,3,12,768]{3,2,1,0:T(8,128)(2,1)}), bf16[32,3,12,768]{3,2,1,0:T(8,128)(2,1)S(1)}, u32[]{:S(2)}, u32[]{:S(2)}) %all-to-all-start) | async-done | bytes 1769504 | tf_op jit(solution)/shard_map/all_to_all | solution.py:60
  128.1 2.1 reshape.52
  134.0 1.8 fusion.9
  137.2 2.3 convolution_convert_fusion.2
  139.5 2.4 convolution_convert_fusion.1
  141.9 2.4 convolution_convert_fusion.3
  144.3 1.9 fusion.2
  146.2 84.8 %fusion = bf16[16,1152]{1,0:T(8,128)(2,1)S(1)} fusion(bf16[384,1152]{1,0:T(8,128)(2,1)S(1)} %fusion.2), kind=kCustom, calls=%all-reduce-scatter | all-reduce-scatter fusion | flops 589825 | bytes 923648
  231.1 3.5 %collective-permute-start.1 = (bf16[16,1152]{1,0:T(8,128)(2,1)S(1)}, bf16[16,1152]{1,0:T(8,128)(2,1)S(1)}, u32[]{:S(2)}, u32[]{:S(2)}) collective-permute-start(bf16[16,1152]{1,0:T(8,128)(2,1)S(1)} %fusion), channel_id=1, source_target_pairs={{0,16},{16,32},{32,48},{48,64},{64,80},{80,96},{96,112},{112,128},... | collective-permute-start | bytes 110600
  234.5 1.9 collective-permute-start.2
  236.5 1.9 collective-permute-start.3
  238.4 1.9 collective-permute-start.4
  240.3 2.0 fusion.19
  242.4 10.7 %collective-permute-start.8 = (bf16[12,1152]{1,0:T(8,128)(2,1)S(1)}, bf16[12,1152]{1,0:T(8,128)(2,1)S(1)}, u32[]{:S(2)}, u32[]{:S(2)}) collective-permute-start(bf16[12,1152]{1,0:T(8,128)(2,1)S(1)} %slice.37), channel_id=1, source_target_pairs={{0,128},{16,144},{32,160},{48,176},{64,192},{80,208},{96,224},{112... | collective-permute-start | bytes 82952
  253.1 7.0 %collective-permute-done.8 = bf16[12,1152]{1,0:T(8,128)(2,1)S(1)} collective-permute-done((bf16[12,1152]{1,0:T(8,128)(2,1)S(1)}, bf16[12,1152]{1,0:T(8,128)(2,1)S(1)}, u32[]{:S(2)}, u32[]{:S(2)}) %collective-permute-start.8) | collective-permute-done | bytes 27680
  260.1 10.7 %collective-permute-start.5 = (bf16[16,1152]{1,0:T(8,128)(2,1)S(1)}, bf16[16,1152]{1,0:T(8,128)(2,1)S(1)}, u32[]{:S(2)}, u32[]{:S(2)}) collective-permute-start(bf16[16,1152]{1,0:T(8,128)(2,1)S(1)} %fusion), channel_id=1, source_target_pairs={{0,80},{16,96},{32,112},{48,128},{64,144},{80,160},{96,176},{112,1... | collective-permute-start | bytes 110600
  270.9 2.4 collective-permute-start.6
  273.3 1.9 collective-permute-start.7
  276.2 9.8 %collective-permute-done.6 = bf16[16,1152]{1,0:T(8,128)(2,1)S(1)} collective-permute-done((bf16[16,1152]{1,0:T(8,128)(2,1)S(1)}, bf16[16,1152]{1,0:T(8,128)(2,1)S(1)}, u32[]{:S(2)}, u32[]{:S(2)}) %collective-permute-start.6) | collective-permute-done | bytes 36896
  286.0 3.3 collective-permute-done.7
  290.8 53.0 %all-reduce.4 = bf16[12,1152]{1,0:T(8,128)(2,1)S(1)} all-reduce(bf16[12,1152]{1,0:T(8,128)(2,1)S(1)} %constant_dynamic-slice_fusion), channel_id=3, replica_groups=mesh['dp'=32,'tm'=16] {'tm'}, use_global_device_ids=true, to_apply=%region_6.0.clone | all-reduce | flops 13824 | bytes 55296
  (54 shorter events, 16.2 us)
Async XLA Ops:
  0.6 27.2 %copy-start = (bf16[384,1152]{1,0:T(8,128)(2,1)S(1)}, bf16[384,1152]{1,0:T(8,128)(2,1)}, u32[]{:S(2)}) copy-start(bf16[384,1152]{1,0:T(8,128)(2,1)} %param.8) | copy-start | bytes 2654212
  3.2 24.7 %copy-start.11 = (f32[384]{0:T(512)S(1)}, f32[384]{0:T(512)}, u32[]{:S(2)}) copy-start(f32[384]{0:T(512)} %param.7) | copy-start | bytes 4612
  3.2 123.4 %all-to-all-start = ((bf16[32,3,12,768]{3,2,1,0:T(8,128)(2,1)}), bf16[32,3,12,768]{3,2,1,0:T(8,128)(2,1)S(1)}, u32[]{:S(2)}, u32[]{:S(2)}) async-start(bf16[32,3,12,768]{3,2,1,0:T(8,128)(2,1)} %stack.2), calls=%async_computation | async-start | bytes 4718592 | tf_op jit(solution)/shard_map/all_to_all | solution.py:60
  21.5 110.8 %collective-permute-start = (bf16[2,256,768]{2,1,0:T(8,128)(2,1)}, bf16[2,256,768]{2,1,0:T(8,128)(2,1)}, u32[]{:S(2)}, u32[]{:S(2)}) collective-permute-start(bf16[2,256,768]{2,1,0:T(8,128)(2,1)} %bitcast.52), channel_id=1, source_target_pairs={{1,0},{2,1},{3,2},{4,3},{5,4},{6,5},{7,6},{8,7},{9,8},{10,9},{11,1... | collective-permute-start | bytes 2359304 | tf_op jit(solution)/shard_map/ppermute | solution.py:11
  29.8 1.4 copy-start.6
  30.1 1.1 copy-start.4
  128.0 2.1 copy-start.2
  128.1 2.3 copy-start.1
  130.5 1.9 copy-start.8
  130.5 1.9 copy-start.9
  133.9 1.9 copy-start.10
  134.0 2.3 copy-start.7
  135.8 1.0 copy-start.3
  141.9 2.4 copy-start.5
  141.9 2.4 copy-start.12
  231.1 39.8 %collective-permute-start.1 = (bf16[16,1152]{1,0:T(8,128)(2,1)S(1)}, bf16[16,1152]{1,0:T(8,128)(2,1)S(1)}, u32[]{:S(2)}, u32[]{:S(2)}) collective-permute-start(bf16[16,1152]{1,0:T(8,128)(2,1)S(1)} %fusion), channel_id=1, source_target_pairs={{0,16},{16,32},{32,48},{48,64},{64,80},{80,96},{96,112},{112,128},... | collective-permute-start | bytes 110600
  234.5 38.7 %collective-permute-start.2 = (bf16[16,1152]{1,0:T(8,128)(2,1)S(1)}, bf16[16,1152]{1,0:T(8,128)(2,1)S(1)}, u32[]{:S(2)}, u32[]{:S(2)}) collective-permute-start(bf16[16,1152]{1,0:T(8,128)(2,1)S(1)} %fusion), channel_id=1, source_target_pairs={{0,32},{16,48},{32,64},{48,80},{64,96},{80,112},{96,128},{112,144}... | collective-permute-start | bytes 110600
  236.5 39.7 %collective-permute-start.3 = (bf16[16,1152]{1,0:T(8,128)(2,1)S(1)}, bf16[16,1152]{1,0:T(8,128)(2,1)S(1)}, u32[]{:S(2)}, u32[]{:S(2)}) collective-permute-start(bf16[16,1152]{1,0:T(8,128)(2,1)S(1)} %fusion), channel_id=1, source_target_pairs={{0,48},{16,64},{32,80},{48,96},{64,112},{80,128},{96,144},{112,160... | collective-permute-start | bytes 110600
  238.4 37.8 %collective-permute-start.4 = (bf16[16,1152]{1,0:T(8,128)(2,1)S(1)}, bf16[16,1152]{1,0:T(8,128)(2,1)S(1)}, u32[]{:S(2)}, u32[]{:S(2)}) collective-permute-start(bf16[16,1152]{1,0:T(8,128)(2,1)S(1)} %fusion), channel_id=1, source_target_pairs={{0,64},{16,80},{32,96},{48,112},{64,128},{80,144},{96,160},{112,17... | collective-permute-start | bytes 110600
  242.4 17.7 %collective-permute-start.8 = (bf16[12,1152]{1,0:T(8,128)(2,1)S(1)}, bf16[12,1152]{1,0:T(8,128)(2,1)S(1)}, u32[]{:S(2)}, u32[]{:S(2)}) collective-permute-start(bf16[12,1152]{1,0:T(8,128)(2,1)S(1)} %slice.37), channel_id=1, source_target_pairs={{0,128},{16,144},{32,160},{48,176},{64,192},{80,208},{96,224},{112... | collective-permute-start | bytes 82952
  260.1 16.1 %collective-permute-start.5 = (bf16[16,1152]{1,0:T(8,128)(2,1)S(1)}, bf16[16,1152]{1,0:T(8,128)(2,1)S(1)}, u32[]{:S(2)}, u32[]{:S(2)}) collective-permute-start(bf16[16,1152]{1,0:T(8,128)(2,1)S(1)} %fusion), channel_id=1, source_target_pairs={{0,80},{16,96},{32,112},{48,128},{64,144},{80,160},{96,176},{112,1... | collective-permute-start | bytes 110600
  270.9 15.2 %collective-permute-start.6 = (bf16[16,1152]{1,0:T(8,128)(2,1)S(1)}, bf16[16,1152]{1,0:T(8,128)(2,1)S(1)}, u32[]{:S(2)}, u32[]{:S(2)}) collective-permute-start(bf16[16,1152]{1,0:T(8,128)(2,1)S(1)} %fusion), channel_id=1, source_target_pairs={{0,96},{16,112},{32,128},{48,144},{64,160},{80,176},{96,192},{112,... | collective-permute-start | bytes 110600
  273.3 16.1 %collective-permute-start.7 = (bf16[16,1152]{1,0:T(8,128)(2,1)S(1)}, bf16[16,1152]{1,0:T(8,128)(2,1)S(1)}, u32[]{:S(2)}, u32[]{:S(2)}) collective-permute-start(bf16[16,1152]{1,0:T(8,128)(2,1)S(1)} %fusion), channel_id=1, source_target_pairs={{0,112},{16,128},{32,144},{48,160},{64,176},{80,192},{96,208},{112... | collective-permute-start | bytes 110600
